TPU v7x, 32 devices: a whole 2x2x4 slice. The times are simulated.
32 devices in a mesh: groups: 2 (over y), tm: 4 (over z), mp: 4 (over x, core).
Axes of the slice: x: 2, y: 2, z: 4, core: 2. Of those that a mesh axis runs over, the one named last changes fastest.
Arguments:
- waveform: float32 [1310720], P(('groups', 'tm', 'mp')), parts along dimension 0, may hold values from -0.8 to 0.8
- segment_start: int32 [2048], P(('groups', 'tm')), parts along dimension 0, may hold values from 0 to 1023, as said below
- segment_end: int32 [2048], P(('groups', 'tm')), parts along dimension 0, may hold values from 1 to 1024, as said below
- w_subsample: bfloat16 [512, 1536], replicated, may hold values from -0.25 to 0.25
- w_attention: bfloat16 [3, 1536, 1536], P(None, None, 'mp')
- w_output: bfloat16 [1536, 1536], P('mp'), may hold values from -0.15625 to 0.15625
- gain_convolution: float32 [1536], replicated, may hold values from 0.1 to 1.9
- w_depthwise: bfloat16 [31, 1536], replicated, may hold values from -1 to 1
Outputs:
- encoded: bfloat16 [2048, 1536], P(('groups', 'tm', 'mp')), parts along dimension 0
There are 2 independent parts, one for each index of `groups`. A program takes and returns all parts, laid end to end along the dimension named above; an argument that names none is the same for every part. Nothing has to cross between parts.
Inputs may be any that keep to these rules, and one draw needn't show every extreme that they name: Segments are contiguous runs of frames that tile the slab: segment_start[i] <= i < segment_end[i], and all frames of a run share both values; every run has 150 to 750 frames except the first and the last, which may be shorter; one run of exactly 750 frames lies in every draw. `segment_end`: the end of the run holding each frame, as described for segment_start.
All inputs are finite; a program needn't handle non-finite values.
Results may differ from a plain program's by a relative error of at most 0.015.
Values may be sent and summed in bfloat16 or wider, within the bound.
A program may use at most 64 MiB of HBM per device.

v0:
```python
import math

import jax
import jax.numpy as jnp
from jax import lax
from jax.sharding import PartitionSpec as P

HD = 64
NMEL = 128
NFFT = 400
HOP = 160
BINS = 256
SUB = 4
KERNEL = 31
SEG_MAX = 750


def shifted(block, axis, distance):
    devices = range(lax.axis_size(axis))
    route = [(i - distance, i) for i in devices if i - distance in devices]
    return lax.ppermute(block, axis, route)


def with_halo(cells, sides, width):
    for axis, dim in sides:
        count = lax.axis_size(axis)
        ends = count - 1
        head = lax.slice_in_dim(cells, 0, width, axis=dim)
        tail = lax.slice_in_dim(cells, cells.shape[dim] - width, cells.shape[dim], axis=dim)
        cells = jnp.concatenate(
            [
                lax.ppermute(tail, axis, [(i, (i + 1) % count) for i in range(ends)]),
                cells,
                lax.ppermute(head, axis, [((i + 1) % count, i) for i in range(ends)]),
            ],
            axis=dim,
        )
    return cells


def fourier_table():
    sample_index = jnp.arange(NFFT, dtype=jnp.int32)[:, None]
    bin_index = jnp.arange(BINS, dtype=jnp.int32)[None, :]
    phase_int = sample_index * bin_index % NFFT
    angle_rad = phase_int.astype(jnp.float32) * (2.0 * math.pi / NFFT)
    window_row = 0.5 - 0.5 * jnp.cos(jnp.arange(NFFT, dtype=jnp.float32) * (2.0 * math.pi / NFFT))
    kept_bins = bin_index <= NFFT // 2
    cosine_part = jnp.where(kept_bins, jnp.cos(angle_rad), 0.0) * window_row[:, None]
    sine_part = jnp.where(kept_bins, -jnp.sin(angle_rad), 0.0) * window_row[:, None]
    return jnp.concatenate([cosine_part, sine_part], axis=1)


def mel_bank():
    mel_top = 2595.0 * math.log10(1.0 + 8000.0 / 700.0)
    mel_points = jnp.arange(NMEL + 2, dtype=jnp.float32) * (mel_top / (NMEL + 1))
    hertz_points = 700.0 * (jnp.power(10.0, mel_points / 2595.0) - 1.0)
    edges = hertz_points * (NFFT / 16000.0)
    centers = edges[1:-1]
    widths = jnp.maximum(edges[2:] - edges[1:-1], 1.0)
    bin_value = jnp.arange(BINS, dtype=jnp.float32)[:, None]
    triangle = jnp.maximum(0.0, 1.0 - jnp.abs(bin_value - centers[None, :]) / widths[None, :])
    return jnp.where(bin_value <= NFFT // 2, triangle, 0.0)


def frame_rows(padded, frame_count):
    blocks_needed = -(-NFFT // HOP)
    blocks = padded.reshape(frame_count + blocks_needed - 1, HOP)
    pieces = [blocks[offset : offset + frame_count] for offset in range(blocks_needed)]
    return jnp.concatenate(pieces, axis=1)[:, :NFFT]


def log_mel(frames):
    spectrum = jnp.dot(
        frames, fourier_table(), precision=lax.Precision.HIGHEST, preferred_element_type=jnp.float32
    )
    spectral_power = jnp.square(spectrum[:, :BINS]) + jnp.square(spectrum[:, BINS:])
    energy = jnp.dot(
        spectral_power,
        mel_bank(),
        precision=lax.Precision.HIGHEST,
        preferred_element_type=jnp.float32,
    )
    return jnp.log(energy + 1e-06)


def normalize(values):
    values = values.astype(jnp.float32)
    center = jnp.mean(values, axis=-1, keepdims=True)
    spread = jnp.mean(jnp.square(values - center), axis=-1, keepdims=True)
    return (values - center) * lax.rsqrt(spread + 1e-05)


def layer_norm(values, gain_row):
    return normalize(values) * gain_row


def fold_keys(state, pair_block, positions, queries, starts, finish):
    running_max, denominator, numerator = state
    row_count = pair_block.shape[0]
    heads_local = queries.shape[1]
    local_width = heads_local * HD
    key_block = pair_block[:, :local_width].reshape(row_count, heads_local, HD)
    value_block = pair_block[:, local_width:].reshape(row_count, heads_local, HD)
    scores = jnp.einsum("qhd,khd->qhk", queries, key_block, preferred_element_type=jnp.float32) * (
        1.0 / math.sqrt(HD)
    )
    allowed = (positions[None, :] >= starts[:, None]) & (positions[None, :] < finish[:, None])
    scores = jnp.where(allowed[:, None, :], scores, -1e30)
    new_max = jnp.maximum(running_max, jnp.max(scores, axis=-1))
    weights = jnp.exp(scores - new_max[..., None])
    factor = jnp.exp(running_max - new_max)
    denominator = denominator * factor + jnp.sum(weights, axis=-1)
    numerator = numerator * factor[..., None] + jnp.einsum(
        "qhk,khd->qhd",
        weights.astype(jnp.bfloat16),
        value_block,
        preferred_element_type=jnp.float32,
    )
    return (new_max, denominator, numerator)


def shards(
    waveform,
    segment_start,
    segment_end,
    w_subsample,
    w_attention,
    w_output,
    gain_convolution,
    w_depthwise,
):
    frames_local = waveform.shape[0] // (SUB * HOP)
    frames_shard = segment_start.shape[0]
    local_width = w_attention.shape[2]
    heads_local = local_width // HD
    time_index = lax.axis_index("tm")
    model_index = lax.axis_index("mp")
    blocks_needed = -(-NFFT // HOP)
    next_samples = shifted(waveform[: NFFT - HOP], ("tm", "mp"), -1)
    tail_zeros = jnp.zeros((blocks_needed * HOP - NFFT,), waveform.dtype)
    padded = jnp.concatenate([waveform, next_samples, tail_zeros])
    stacked = (
        log_mel(frame_rows(padded, frames_local * SUB))
        .reshape(frames_local, SUB * NMEL)
        .astype(jnp.bfloat16)
    )
    all_stacked = lax.all_gather(stacked, "mp", axis=0, tiled=True)
    all_features = jnp.dot(all_stacked, w_subsample, preferred_element_type=jnp.float32).astype(
        jnp.bfloat16
    )
    features = lax.dynamic_slice_in_dim(all_features, model_index * frames_local, frames_local, 0)
    portion = normalize(all_features).astype(jnp.bfloat16)
    mapped = jnp.einsum("rd,kdc->rkc", portion, w_attention, preferred_element_type=jnp.float32)
    projected = mapped.astype(jnp.bfloat16).reshape(portion.shape[0], 3 * local_width)
    queries = projected[:, :local_width].reshape(frames_shard, heads_local, HD)
    pair_rows = projected[:, local_width:]
    own_positions = time_index * frames_shard + jnp.arange(frames_shard, dtype=jnp.int32)
    state = (
        jnp.full((frames_shard, heads_local), -1e30, jnp.float32),
        jnp.zeros((frames_shard, heads_local), jnp.float32),
        jnp.zeros((frames_shard, heads_local, HD), jnp.float32),
    )
    state = fold_keys(state, pair_rows, own_positions, queries, segment_start, segment_end)
    reach_shards = min((SEG_MAX - 2) // frames_shard + 1, lax.axis_size("tm") - 1)
    for distance in range(1, reach_shards + 1):
        for leftward in (True, False):
            shift_by = distance if leftward else -distance
            arrived = shifted(pair_rows, "tm", shift_by)
            positions = (time_index - shift_by) * frames_shard + jnp.arange(
                frames_shard, dtype=jnp.int32
            )
            state = fold_keys(state, arrived, positions, queries, segment_start, segment_end)
    running_max, denominator, numerator = state
    attended = (
        (numerator / denominator[..., None]).reshape(frames_shard, local_width).astype(jnp.bfloat16)
    )
    branch = lax.psum_scatter(
        jnp.dot(attended, w_output, preferred_element_type=jnp.float32).astype(jnp.bfloat16),
        "mp",
        scatter_dimension=0,
        tiled=True,
    ).astype(jnp.float32)
    mixed_rows = (features.astype(jnp.float32) + branch).astype(jnp.bfloat16)
    conv_input = layer_norm(mixed_rows, gain_convolution).astype(jnp.bfloat16)
    half_kernel = KERNEL // 2
    haloed = with_halo(conv_input, ((("tm", "mp"), 0),), half_kernel)
    convolved = jnp.zeros((frames_local, conv_input.shape[1]), jnp.float32)
    for tap_index in range(KERNEL):
        convolved = convolved + haloed[tap_index : tap_index + frames_local].astype(
            jnp.float32
        ) * w_depthwise[tap_index].astype(jnp.float32)
    return (mixed_rows.astype(jnp.float32) + jax.nn.silu(convolved)).astype(jnp.bfloat16)


def solution(mesh):
    placed = (
        P(("groups", "tm", "mp")),
        P(("groups", "tm")),
        P(("groups", "tm")),
        P(),
        P(None, None, "mp"),
        P("mp", None),
        P(),
        P(),
    )
    return jax.shard_map(
        shards,
        mesh=mesh,
        in_specs=placed,
        out_specs=P(("groups", "tm", "mp"), None),
        check_vma=False,
    )
```

profile of v0, /device:TPU:1, one launch (start us, length us, event | category | flops | bytes accessed | tf_op | source)
XLA Modules:
  0.0 141.9 jit_solution(2434125317610870211)
XLA Ops:
  6.5 0.8 slice.318
  7.4 2.0 %collective-permute-start = (f32[240]{0:T(256)S(1)}, f32[240]{0:T(256)S(1)}, u32[]{:S(2)}, u32[]{:S(2)}) collective-permute-start(f32[240]{0:T(256)S(1)} %slice.318), channel_id=1, source_target_pairs={{1,0},{2,1},{3,2},{4,3},{5,4},{6,5},{7,6},{8,7},{9,8},{10,9},{11,1... | collective-permute-start | bytes 2888 | tf_op jit(solution)/shard_map/ppermute | solution.py:21
  9.5 0.5 iota_compare_fusion.1
  10.0 0.7 fusion.125
  10.7 3.2 %select_multiply_fusion.1 = (f32[400,256]{1,0:T(8,128)}, f32[400,256]{1,0:T(8,128)}) fusion(f32[400]{0:T(512)S(1)} %multiply_subtract_fusion, pred[256]{0:T(512)(128)(4,1)} %iota_compare_fusion.1), kind=kLoop, calls=%fused_computation.116 | loop fusion | flops 1433600 | bytes 821056 | tf_op jit(solution)/shard_map/mul | solution.py:48
  13.9 1.9 %compare_and_fusion.6 = (pred[256,256]{0,1:T(8,128)(4,1)}, pred[256,256]{0,1:T(8,128)(4,1)}, pred[256,256]{0,1:T(8,128)(4,1)}, pred[256,256]{0,1:T(8,128)(4,1)},...) fusion(s32[256]{0:T(256)} %param.10, s32[256]{0:T(256)} %param.9, ...), kind=kLoop, calls=%fused_computation.135 | loop fusion | flops 1376256 | bytes 467968 | tf_op jit(solution)/shard_map/and | solution.py:107
  15.8 1.8 %slice.317 = f32[256,160]{1,0:T(8,128)} reshape(f32[40960]{0:T(1024)} %param.8) | data formatting | bytes 327680 | tf_op jit(solution)/shard_map/slice | solution.py:68
  17.5 1.7 %concatenate.48 = f32[41280]{0:T(1024)} concatenate(f32[40960]{0:T(1024)} %param.8, f32[240]{0:T(256)S(1)} %collective-permute-done, f32[80]{0:T(128)S(1)} %broadcast_in_dim.82), dimensions={0} | concatenate | bytes 330240 | tf_op jit(solution)/shard_map/concatenate | solution.py:141
  19.2 1.7 %slice.407 = f32[40960]{0:T(1024)} slice(f32[41280]{0:T(1024)} %concatenate.48), slice={[320:41280]} | slice | bytes 327680 | tf_op jit(solution)/shard_map/slice | solution.py:68
  20.9 1.8 %slice.322 = f32[256,160]{1,0:T(8,128)} reshape(f32[40960]{0:T(1024)} %slice.407) | data formatting | bytes 327680 | tf_op jit(solution)/shard_map/slice | solution.py:68
  22.7 1.7 %pad_maximum_fusion.6 = f32[40960]{0:T(1024)} fusion(f32[240]{0:T(256)S(1)} %collective-permute-done, f32[40960]{0:T(1024)} %param.8), kind=kLoop, calls=%fused_computation.190 | loop fusion | flops 40960 | bytes 328640 | tf_op jit(solution)/shard_map/concatenate | solution.py:141
  24.4 1.8 %slice.320 = f32[256,160]{1,0:T(8,128)} reshape(f32[40960]{0:T(1024)} %pad_maximum_fusion.6) | data formatting | bytes 327680 | tf_op jit(solution)/shard_map/slice | solution.py:68
  26.1 2.5 %fusion.35 = f32[256,512]{1,0:T(8,128)S(1)} fusion(f32[400,256]{1,0:T(8,128)} %get-tuple-element.71, f32[400,256]{1,0:T(8,128)} %get-tuple-element.70, f32[256,160]{1,0:T(8,128)} %slice.322, f32[256,160]{1,0:T(8,128)} %slice.320, f32[256,160]{1,0:T(8,128)} %slice.317), kind=kOutput, calls=%fused_computation.90 | convolution fusion | flops 629555200 | bytes 1835008 | tf_op jit(solution)/shard_map/dot_general | solution.py:73
  28.6 1.1 fusion.34
  29.7 1.5 %convert_element_type.229 = bf16[64,512]{1,0:T(8,128)(2,1)} reshape(bf16[256,128]{1,0:T(8,128)(2,1)} %fusion.34) | data formatting | bytes 131072 | tf_op jit(solution)/shard_map/convert_element_type | solution.py:145
  31.2 7.3 %all_gather.3 = bf16[256,512]{1,0:T(8,128)(2,1)S(1)} all-gather(bf16[64,512]{1,0:T(8,128)(2,1)} %convert_element_type.229), channel_id=1, replica_groups=mesh['groups'=2,'tm'=4,'mp'=4] {'mp'}, dimensions={0}, use_global_device_ids=true | all-gather | bytes 327680 | tf_op jit(solution)/shard_map/all_gather | solution.py:147
  38.6 2.1 %convert_reduce_fusion = (f32[256]{0:T(256)S(1)}, bf16[256,1536]{1,0:T(8,128)(2,1)S(1)}) fusion(bf16[256,512]{1,0:T(8,128)(2,1)S(1)} %all_gather.3, bf16[512,1536]{1,0:T(8,128)(2,1)} %param.11), kind=kOutput, calls=%fused_computation.3 | convolution fusion | flops 403832576 | bytes 2622464 | tf_op jit(solution)/shard_map/dot_general | solution.py:148
  40.6 0.3 fusion.2
  41.0 0.5 copy-done.1
  41.5 2.1 %convolution_convert_fusion.2 = bf16[256,3,384]{2,0,1:T(8,128)(2,1)} fusion(bf16[3,1536,384]{2,1,0:T(8,128)(2,1)S(1)} %copy-done, bf16[256,1536]{1,0:T(8,128)(2,1)S(1)} %get-tuple-element.82, f32[256]{0:T(256)S(1)} %add_rsqrt_fusion, f32[256]{0:T(256)S(1)} %broadcast_multiply_fusion), kind=kOutput, calls=%fused_computation.36 | convolution fusion | flops 907837440 | bytes 4917248 | tf_op jit(solution)/shard_map/rd,kdc->rkc/dot_general | solution.py:153
  43.6 2.1 %copy.16 = bf16[256,3,384]{0,2,1:T(8,128)(2,1)} copy(bf16[256,3,384]{2,0,1:T(8,128)(2,1)} %convolution_convert_fusion.2) | data formatting | bytes 1179648 | tf_op jit(solution)/shard_map/convert_element_type | solution.py:154
  45.7 1.1 slice.413
  46.8 5.0 %collective-permute-start.3 = (bf16[256,768]{0,1:T(8,128)(2,1)S(1)}, bf16[256,768]{0,1:T(8,128)(2,1)S(1)}, u32[]{:S(2)}, u32[]{:S(2)}) collective-permute-start(bf16[256,768]{0,1:T(8,128)(2,1)S(1)} %slice.413), channel_id=1, source_target_pairs={{0,8},{4,12},{1,9},{5,13},{2,10},{6,14},{3,11},{7,15},{16,24},{20,... | collective-permute-start | bytes 1179656 | tf_op jit(solution)/shard_map/ppermute | solution.py:21
  51.8 1.2 fusion.117
  53.0 1.4 %collective-permute-start.2 = (bf16[256,768]{0,1:T(8,128)(2,1)S(1)}, bf16[256,768]{0,1:T(8,128)(2,1)S(1)}, u32[]{:S(2)}, u32[]{:S(2)}) collective-permute-start(bf16[256,768]{0,1:T(8,128)(2,1)S(1)} %slice.413), channel_id=1, source_target_pairs={{4,0},{8,4},{12,8},{5,1},{9,5},{13,9},{6,2},{10,6},{14,10},{7,3},{... | collective-permute-start | bytes 1179656 | tf_op jit(solution)/shard_map/ppermute | solution.py:21
  54.4 4.0 %collective-permute-start.1 = (bf16[256,768]{0,1:T(8,128)(2,1)S(1)}, bf16[256,768]{0,1:T(8,128)(2,1)S(1)}, u32[]{:S(2)}, u32[]{:S(2)}) collective-permute-start(bf16[256,768]{0,1:T(8,128)(2,1)S(1)} %slice.413), channel_id=1, source_target_pairs={{0,4},{4,8},{8,12},{1,5},{5,9},{9,13},{2,6},{6,10},{10,14},{3,7},{... | collective-permute-start | bytes 1179656 | tf_op jit(solution)/shard_map/ppermute | solution.py:21
  58.4 1.3 collective-permute-start.4
  59.7 5.9 %collective-permute-start.5 = (bf16[256,768]{0,1:T(8,128)(2,1)S(1)}, bf16[256,768]{0,1:T(8,128)(2,1)S(1)}, u32[]{:S(2)}, u32[]{:S(2)}) collective-permute-start(bf16[256,768]{0,1:T(8,128)(2,1)S(1)} %slice.413), channel_id=1, source_target_pairs={{0,12},{1,13},{2,14},{3,15},{16,28},{17,29},{18,30},{19,31}} | collective-permute-start | bytes 1179656 | tf_op jit(solution)/shard_map/ppermute | solution.py:21
  65.6 0.4 fusion.132
  66.1 1.5 %collective-permute-start.6 = (bf16[256,768]{0,1:T(8,128)(2,1)S(1)}, bf16[256,768]{0,1:T(8,128)(2,1)S(1)}, u32[]{:S(2)}, u32[]{:S(2)}) collective-permute-start(bf16[256,768]{0,1:T(8,128)(2,1)S(1)} %slice.413), channel_id=1, source_target_pairs={{12,0},{13,1},{14,2},{15,3},{28,16},{29,17},{30,18},{31,19}} | collective-permute-start | bytes 1179656 | tf_op jit(solution)/shard_map/ppermute | solution.py:21
  67.6 0.5 fusion.129
  68.2 0.3 copy-done.7
  68.5 0.4 fusion.130
  69.0 0.4 fusion.131
  69.5 22.0 %collective-permute-done.4 = bf16[256,768]{0,1:T(8,128)(2,1)S(1)} collective-permute-done((bf16[256,768]{0,1:T(8,128)(2,1)S(1)}, bf16[256,768]{0,1:T(8,128)(2,1)S(1)}, u32[]{:S(2)}, u32[]{:S(2)}) %collective-permute-start.4) | collective-permute-done | bytes 393248 | tf_op jit(solution)/shard_map/ppermute | solution.py:21
  91.5 0.4 fusion.128
  92.1 0.3 copy-done.4
  92.4 0.4 fusion.127
  92.9 0.4 fusion.126
  93.4 0.2 fusion.8
  93.6 0.4 convolution_bitcast_fusion.4
  94.0 0.2 fusion.10
  94.2 0.4 convolution_bitcast_fusion.3
  94.6 0.2 fusion.12
  94.8 0.4 convolution_bitcast_fusion.2
  95.2 0.2 fusion.14
  95.4 0.4 convolution_bitcast_fusion.1
  95.8 0.2 fusion.16
  96.0 0.4 convolution_bitcast_fusion
  96.4 0.2 fusion.4
  96.6 0.2 fusion.6
  96.9 0.4 fusion.19
  97.3 0.4 fusion.32
  97.7 0.8 copy-done.2
  98.6 1.5 %convolution_convert_fusion = bf16[256,1536]{1,0:T(8,128)(2,1)} fusion(bf16[256,384]{0,1:T(8,128)(2,1)S(1)} %bitcast.113, bf16[384,1536]{1,0:T(8,128)(2,1)S(1)} %copy-done.2), kind=kOutput, calls=%fused_computation | convolution fusion | flops 302383104 | bytes 2162688 | tf_op jit(solution)/shard_map/dot_general | solution.py:178
  100.1 2.3 %convert_reduce_fusion.32 = (f32[1536]{0:T(1024)S(1)}, f32[1536]{0:T(1024)S(1)}, f32[1536]{0:T(1024)}, f32[1536]{0:T(1024)}, f32[1536]{0:T(1024)}, /*index=5*/f3...) fusion(bf16[31,1536]{1,0:T(8,128)(2,1)} %param.15), kind=kLoop, calls=%fused_computation.241 | loop fusion | flops 29184 | bytes 175104 | tf_op jit(solution)/shard_map/mul | solution.py:189
  102.4 19.2 %reduce-scatter.2.cloned.1.call-done = bf16[64,1536]{1,0:T(8,128)(2,1)} async-done(((bf16[256,1536]{1,0:T(8,128)(2,1)}), bf16[64,1536]{1,0:T(8,128)(2,1)}) %reduce-scatter.2.cloned.1.call-update) | async-done | bytes 196624 | tf_op jit(solution)/shard_map/reduce_scatter | solution.py:177
  121.7 1.3 convert_reduce_fusion.1
  123.2 0.8 fusion.67
  124.1 2.7 %collective-permute-start.7 = (bf16[15,1536]{1,0:T(8,128)(2,1)S(1)}, bf16[15,1536]{1,0:T(8,128)(2,1)S(1)}, u32[]{:S(2)}, u32[]{:S(2)}) collective-permute-start(bf16[15,1536]{1,0:T(8,128)(2,1)S(1)} %get-tuple-element.66), channel_id=1, source_target_pairs={{0,1},{1,2},{2,3},{3,4},{4,5},{5,6},{6,7},{7,8},{8,9},{9,10},{10,1... | collective-permute-start | bytes 138248 | tf_op jit(solution)/shard_map/ppermute | solution.py:32
  126.8 1.9 %collective-permute-start.8 = (bf16[15,1536]{1,0:T(8,128)(2,1)S(1)}, bf16[15,1536]{1,0:T(8,128)(2,1)S(1)}, u32[]{:S(2)}, u32[]{:S(2)}) collective-permute-start(bf16[15,1536]{1,0:T(8,128)(2,1)S(1)} %get-tuple-element.67), channel_id=1, source_target_pairs={{1,0},{2,1},{3,2},{4,3},{5,4},{6,5},{7,6},{8,7},{9,8},{10,9},{11,1... | collective-permute-start | bytes 138248 | tf_op jit(solution)/shard_map/ppermute | solution.py:34
  128.7 1.3 convert_reduce_fusion.31
  130.0 2.2 %collective-permute-done.8 = bf16[15,1536]{1,0:T(8,128)(2,1)S(1)} collective-permute-done((bf16[15,1536]{1,0:T(8,128)(2,1)S(1)}, bf16[15,1536]{1,0:T(8,128)(2,1)S(1)}, u32[]{:S(2)}, u32[]{:S(2)}) %collective-permute-start.8) | collective-permute-done | bytes 46112 | tf_op jit(solution)/shard_map/ppermute | solution.py:34
  132.3 2.7 %fusion.68 = bf16[64,1536]{1,0:T(8,128)(2,1)} fusion(bf16[64,1536]{1,0:T(8,128)(2,1)S(1)} %get-tuple-element.37, bf16[64,1536]{1,0:T(8,128)(2,1)S(1)} %fusion.67, bf16[15,1536]{1,0:T(8,128)(2,1)S(1)} %collective-permute-done.8, bf16[15,1536]{1,0:T(8,128)(2,1)S(1)} %collective-permute-done.7, f32[1536]{0:T(1024)S(1)} %get-tuple-element.34, ...), kind=kLoop, calls=%fused_computation.124 | loop fusion | flops 18579456 | bytes 872448 | tf_op jit(solution)/shard_map/convert_element_type | solution.py:192
  (85 shorter events, 0.8 us)
Async XLA Ops:
  6.5 35.0 %copy-start = (bf16[3,1536,384]{2,1,0:T(8,128)(2,1)S(1)}, bf16[3,1536,384]{2,1,0:T(8,128)(2,1)}, u32[]{:S(2)}) copy-start(bf16[3,1536,384]{2,1,0:T(8,128)(2,1)} %param.12) | copy-start | bytes 10616836
  6.5 115.0 %reduce-scatter.2.cloned.1.call-start = ((), (), s32[]{:S(2)}) async-start(), calls=%async_computation.1 | async-start | bytes 983040 | tf_op jit(solution)/shard_map/reduce_scatter | solution.py:177
  7.4 10.1 %collective-permute-start = (f32[240]{0:T(256)S(1)}, f32[240]{0:T(256)S(1)}, u32[]{:S(2)}, u32[]{:S(2)}) collective-permute-start(f32[240]{0:T(256)S(1)} %slice.318), channel_id=1, source_target_pairs={{1,0},{2,1},{3,2},{4,3},{5,4},{6,5},{7,6},{8,7},{9,8},{10,9},{11,1... | collective-permute-start | bytes 2888 | tf_op jit(solution)/shard_map/ppermute | solution.py:21
  20.9 7.7 %copy-start.27 = (f32[128]{0:T(128)S(1)}, f32[128]{0:T(128)}, u32[]{:S(2)}) copy-start(f32[128]{0:T(128)} %get-tuple-element.79) | copy-start | bytes 1540
  20.9 7.7 %copy-start.28 = (f32[128]{0:T(128)S(1)}, f32[128]{0:T(128)}, u32[]{:S(2)}) copy-start(f32[128]{0:T(128)} %get-tuple-element.80) | copy-start | bytes 1540
  40.6 0.9 copy-start.1
  45.7 19.9 %copy-start.9 = (pred[256,256]{0,1:T(8,128)(4,1)S(1)}, pred[256,256]{0,1:T(8,128)(4,1)}, u32[]{:S(2)}) copy-start(pred[256,256]{0,1:T(8,128)(4,1)} %get-tuple-element.72) | copy-start | bytes 196612
  46.8 19.3 %collective-permute-start.3 = (bf16[256,768]{0,1:T(8,128)(2,1)S(1)}, bf16[256,768]{0,1:T(8,128)(2,1)S(1)}, u32[]{:S(2)}, u32[]{:S(2)}) collective-permute-start(bf16[256,768]{0,1:T(8,128)(2,1)S(1)} %slice.413), channel_id=1, source_target_pairs={{0,8},{4,12},{1,9},{5,13},{2,10},{6,14},{3,11},{7,15},{16,24},{20,... | collective-permute-start | bytes 1179656 | tf_op jit(solution)/shard_map/ppermute | solution.py:21
  52.9 14.7 %copy-start.8 = (pred[256,256]{0,1:T(8,128)(4,1)S(1)}, pred[256,256]{0,1:T(8,128)(4,1)}, u32[]{:S(2)}) copy-start(pred[256,256]{0,1:T(8,128)(4,1)} %get-tuple-element.75) | copy-start | bytes 196612
  53.0 15.2 %collective-permute-start.2 = (bf16[256,768]{0,1:T(8,128)(2,1)S(1)}, bf16[256,768]{0,1:T(8,128)(2,1)S(1)}, u32[]{:S(2)}, u32[]{:S(2)}) collective-permute-start(bf16[256,768]{0,1:T(8,128)(2,1)S(1)} %slice.413), channel_id=1, source_target_pairs={{4,0},{8,4},{12,8},{5,1},{9,5},{13,9},{6,2},{10,6},{14,10},{7,3},{... | collective-permute-start | bytes 1179656 | tf_op jit(solution)/shard_map/ppermute | solution.py:21
  54.4 14.5 %collective-permute-start.1 = (bf16[256,768]{0,1:T(8,128)(2,1)S(1)}, bf16[256,768]{0,1:T(8,128)(2,1)S(1)}, u32[]{:S(2)}, u32[]{:S(2)}) collective-permute-start(bf16[256,768]{0,1:T(8,128)(2,1)S(1)} %slice.413), channel_id=1, source_target_pairs={{0,4},{4,8},{8,12},{1,5},{5,9},{9,13},{2,6},{6,10},{10,14},{3,7},{... | collective-permute-start | bytes 1179656 | tf_op jit(solution)/shard_map/ppermute | solution.py:21
  58.4 33.1 %collective-permute-start.4 = (bf16[256,768]{0,1:T(8,128)(2,1)S(1)}, bf16[256,768]{0,1:T(8,128)(2,1)S(1)}, u32[]{:S(2)}, u32[]{:S(2)}) collective-permute-start(bf16[256,768]{0,1:T(8,128)(2,1)S(1)} %slice.413), channel_id=1, source_target_pairs={{8,0},{12,4},{9,1},{13,5},{10,2},{14,6},{11,3},{15,7},{24,16},{28,... | collective-permute-start | bytes 1179656 | tf_op jit(solution)/shard_map/ppermute | solution.py:21
  59.7 32.3 %collective-permute-start.5 = (bf16[256,768]{0,1:T(8,128)(2,1)S(1)}, bf16[256,768]{0,1:T(8,128)(2,1)S(1)}, u32[]{:S(2)}, u32[]{:S(2)}) collective-permute-start(bf16[256,768]{0,1:T(8,128)(2,1)S(1)} %slice.413), channel_id=1, source_target_pairs={{0,12},{1,13},{2,14},{3,15},{16,28},{17,29},{18,30},{19,31}} | collective-permute-start | bytes 1179656 | tf_op jit(solution)/shard_map/ppermute | solution.py:21
  66.1 26.7 %collective-permute-start.6 = (bf16[256,768]{0,1:T(8,128)(2,1)S(1)}, bf16[256,768]{0,1:T(8,128)(2,1)S(1)}, u32[]{:S(2)}, u32[]{:S(2)}) collective-permute-start(bf16[256,768]{0,1:T(8,128)(2,1)S(1)} %slice.413), channel_id=1, source_target_pairs={{12,0},{13,1},{14,2},{15,3},{28,16},{29,17},{30,18},{31,19}} | collective-permute-start | bytes 1179656 | tf_op jit(solution)/shard_map/ppermute | solution.py:21
  67.6 0.8 copy-start.7
  68.2 0.8 copy-start.6
  69.0 22.6 %copy-start.5 = (pred[256,256]{0,1:T(8,128)(4,1)S(1)}, pred[256,256]{0,1:T(8,128)(4,1)}, u32[]{:S(2)}) copy-start(pred[256,256]{0,1:T(8,128)(4,1)} %get-tuple-element.76) | copy-start | bytes 196612
  91.5 0.8 copy-start.4
  92.0 0.8 copy-start.3
  97.3 1.3 copy-start.2
  121.5 10.6 %copy-start.10 = (f32[1536]{0:T(1024)S(1)}, f32[1536]{0:T(1024)}, u32[]{:S(2)}) copy-start(f32[1536]{0:T(1024)} %get-tuple-element.7) | copy-start | bytes 18436
  121.5 10.6 %copy-start.11 = (f32[1536]{0:T(1024)S(1)}, f32[1536]{0:T(1024)}, u32[]{:S(2)}) copy-start(f32[1536]{0:T(1024)} %get-tuple-element.8) | copy-start | bytes 18436
  121.5 10.6 %copy-start.12 = (f32[1536]{0:T(1024)S(1)}, f32[1536]{0:T(1024)}, u32[]{:S(2)}) copy-start(f32[1536]{0:T(1024)} %get-tuple-element.9) | copy-start | bytes 18436
  121.5 10.6 %copy-start.13 = (f32[1536]{0:T(1024)S(1)}, f32[1536]{0:T(1024)}, u32[]{:S(2)}) copy-start(f32[1536]{0:T(1024)} %get-tuple-element.10) | copy-start | bytes 18436
  121.5 10.7 %copy-start.14 = (f32[1536]{0:T(1024)S(1)}, f32[1536]{0:T(1024)}, u32[]{:S(2)}) copy-start(f32[1536]{0:T(1024)} %get-tuple-element.11) | copy-start | bytes 18436
  121.5 10.7 %copy-start.15 = (f32[1536]{0:T(1024)S(1)}, f32[1536]{0:T(1024)}, u32[]{:S(2)}) copy-start(f32[1536]{0:T(1024)} %get-tuple-element.12) | copy-start | bytes 18436
  121.6 10.7 %copy-start.16 = (f32[1536]{0:T(1024)S(1)}, f32[1536]{0:T(1024)}, u32[]{:S(2)}) copy-start(f32[1536]{0:T(1024)} %get-tuple-element.13) | copy-start | bytes 18436
  121.6 10.7 %copy-start.17 = (f32[1536]{0:T(1024)S(1)}, f32[1536]{0:T(1024)}, u32[]{:S(2)}) copy-start(f32[1536]{0:T(1024)} %get-tuple-element.14) | copy-start | bytes 18436
  121.6 10.7 %copy-start.18 = (f32[1536]{0:T(1024)S(1)}, f32[1536]{0:T(1024)}, u32[]{:S(2)}) copy-start(f32[1536]{0:T(1024)} %get-tuple-element.15) | copy-start | bytes 18436
  121.6 10.7 %copy-start.19 = (f32[1536]{0:T(1024)S(1)}, f32[1536]{0:T(1024)}, u32[]{:S(2)}) copy-start(f32[1536]{0:T(1024)} %get-tuple-element.16) | copy-start | bytes 18436
  121.6 10.7 %copy-start.20 = (f32[1536]{0:T(1024)S(1)}, f32[1536]{0:T(1024)}, u32[]{:S(2)}) copy-start(f32[1536]{0:T(1024)} %get-tuple-element.17) | copy-start | bytes 18436
  121.6 10.7 %copy-start.21 = (f32[1536]{0:T(1024)S(1)}, f32[1536]{0:T(1024)}, u32[]{:S(2)}) copy-start(f32[1536]{0:T(1024)} %get-tuple-element.18) | copy-start | bytes 18436
  121.6 10.7 %copy-start.22 = (f32[1536]{0:T(1024)S(1)}, f32[1536]{0:T(1024)}, u32[]{:S(2)}) copy-start(f32[1536]{0:T(1024)} %get-tuple-element.19) | copy-start | bytes 18436
  121.6 10.7 %copy-start.23 = (f32[1536]{0:T(1024)S(1)}, f32[1536]{0:T(1024)}, u32[]{:S(2)}) copy-start(f32[1536]{0:T(1024)} %get-tuple-element.20) | copy-start | bytes 18436
  121.6 10.7 %copy-start.24 = (f32[1536]{0:T(1024)S(1)}, f32[1536]{0:T(1024)}, u32[]{:S(2)}) copy-start(f32[1536]{0:T(1024)} %get-tuple-element.21) | copy-start | bytes 18436
  121.6 10.7 %copy-start.25 = (f32[1536]{0:T(1024)S(1)}, f32[1536]{0:T(1024)}, u32[]{:S(2)}) copy-start(f32[1536]{0:T(1024)} %get-tuple-element.22) | copy-start | bytes 18436
  121.7 10.7 %copy-start.26 = (f32[1536]{0:T(1024)S(1)}, f32[1536]{0:T(1024)}, u32[]{:S(2)}) copy-start(f32[1536]{0:T(1024)} %get-tuple-element.23) | copy-start | bytes 18436
  124.1 5.9 %collective-permute-start.7 = (bf16[15,1536]{1,0:T(8,128)(2,1)S(1)}, bf16[15,1536]{1,0:T(8,128)(2,1)S(1)}, u32[]{:S(2)}, u32[]{:S(2)}) collective-permute-start(bf16[15,1536]{1,0:T(8,128)(2,1)S(1)} %get-tuple-element.66), channel_id=1, source_target_pairs={{0,1},{1,2},{2,3},{3,4},{4,5},{5,6},{6,7},{7,8},{8,9},{9,10},{10,1... | collective-permute-start | bytes 138248 | tf_op jit(solution)/shard_map/ppermute | solution.py:32
  126.8 5.4 %collective-permute-start.8 = (bf16[15,1536]{1,0:T(8,128)(2,1)S(1)}, bf16[15,1536]{1,0:T(8,128)(2,1)S(1)}, u32[]{:S(2)}, u32[]{:S(2)}) collective-permute-start(bf16[15,1536]{1,0:T(8,128)(2,1)S(1)} %get-tuple-element.67), channel_id=1, source_target_pairs={{1,0},{2,1},{3,2},{4,3},{5,4},{6,5},{7,6},{8,7},{9,8},{10,9},{11,1... | collective-permute-start | bytes 138248 | tf_op jit(solution)/shard_map/ppermute | solution.py:34
Sparse Core Ops, SparseCore 0:
  100.2 21.2 reduce-scatter.1
where the time goes:
time: 144 us; the launch traced here: 142 us
  waiting for transfers between devices  43.4 us (30%)
  starting transfers between devices  25.8 us (18%)
  other arithmetic  18.7 us (13%)
  local copies, waits for them, and re-layouts  17.6 us (12%)
  matrix products  15 us (10%)
  between operations  14.1 us (10%)
  blocking collectives  7.34 us (5%)
    ppermute x7, waiting for transfers between devices, shifted(): return lax.ppermute(block, axis, route)  22.1 us
    ppermute x7, starting transfers between devices, shifted(): return lax.ppermute(block, axis, route)  21.2 us
    reduce_scatter x1, waiting for transfers between devices, shards(): lax.psum_scatter(jnp.dot(attended, w_output, preferred_element_type=jnp.f...  19.2 us
    all_gather x1, blocking collectives, shards(): all_stacked = lax.all_gather(stacked, 'mp', axis=0, tiled=True)  7.34 us
    slice x4, local copies, waits for them, and re-layouts, frame_rows(): blocks[offset:offset + frame_count]  6.98 us
    mul x2, other arithmetic, shards(): haloed[tap_index:tap_index + frames_local].astype(jnp.float32)  3.57 us
    mul x1, other arithmetic, fourier_table(): jnp.where(kept_bins, jnp.cos(angle_rad), 0.0) * window_row[:, None]  3.21 us
    dot_general x7, matrix products, fold_keys(): jnp.einsum('qhd,khd->qhk', queries, key_block, preferred_element_type=jnp...  3.13 us
  transfers between devices with their start and end apart: 10, of which 3 were waited for; matrix products, arithmetic and copies ran while one was open for 11% of the time, Pallas kernels for 0%

commit v1 on v0

v1 whole, which is shorter than its diff:
```python
import functools
import math

import jax
import jax.numpy as jnp
import numpy as np
from jax import lax
from jax.experimental import pallas as pl
from jax.experimental.pallas import tpu as pltpu
from jax.sharding import PartitionSpec as P

HD = 64
NMEL = 128
NFFT = 400
HOP = 160
BINS = 256
SUB = 4
KERNEL = 31
SEG_MAX = 750
LANES = 128
WIN = 512
EDGE = 16
MESH = pl.DeviceIdType.MESH
F32 = jnp.float32
BF16 = jnp.bfloat16


def fourier_table():
    sample_index = np.arange(NFFT)[:, None]
    bin_index = np.arange(BINS)[None, :]
    angle = (sample_index * bin_index % NFFT) * (2.0 * math.pi / NFFT)
    window = 0.5 - 0.5 * np.cos(np.arange(NFFT) * (2.0 * math.pi / NFFT))
    kept = bin_index <= NFFT // 2
    cosine = np.where(kept, np.cos(angle), 0.0) * window[:, None]
    sine = np.where(kept, -np.sin(angle), 0.0) * window[:, None]
    table = np.concatenate([cosine, sine], axis=1)
    return np.concatenate([table, np.zeros((WIN - NFFT, 2 * BINS))], axis=0)


def mel_bank():
    mel_top = 2595.0 * math.log10(1.0 + 8000.0 / 700.0)
    points = np.arange(NMEL + 2) * (mel_top / (NMEL + 1))
    edges = 700.0 * (np.power(10.0, points / 2595.0) - 1.0) * (NFFT / 16000.0)
    centers = edges[1:-1]
    widths = np.maximum(edges[2:] - edges[1:-1], 1.0)
    bins = np.arange(BINS)[:, None]
    triangle = np.maximum(0.0, 1.0 - np.abs(bins - centers[None, :]) / widths[None, :])
    return np.where(bins <= NFFT // 2, triangle, 0.0)


def halves(values):
    values = values.astype(np.float32)
    high = values.astype(BF16)
    low = (values - high.astype(np.float32)).astype(BF16)
    return np.stack([high, low])


def split(values):
    high = values.astype(BF16)
    return high, (values - high.astype(F32)).astype(BF16)


def wide_dot(values, table):
    high, low = split(values)
    dot = functools.partial(jnp.dot, preferred_element_type=F32)
    return dot(high, table[0]) + (dot(high, table[1]) + dot(low, table[0]))


def flipped(index, bit):
    return index + bit - 2 * bit * ((index // bit) % 2)


def masked_index(index, mask):
    bit = 1
    while bit <= mask:
        if mask & bit:
            index = flipped(index, bit)
        bit *= 2
    return index


def bits_of(count):
    bits = []
    bit = 1
    while bit < count:
        bits.append(bit)
        bit *= 2
    return bits


def low_bit(mask, count):
    return mask & -mask if mask else count


def normalize(values):
    center = jnp.mean(values, axis=-1, keepdims=True)
    shifted = values - center
    spread = jnp.mean(jnp.square(shifted), axis=-1, keepdims=True)
    return shifted * lax.rsqrt(spread + 1e-05)


def beside(t, m, n_t, n_m, step):
    flat = t * n_m + m + step
    return {"tm": flat // n_m, "mp": flat % n_m}


def signal(sem, device):
    pl.semaphore_signal(sem, inc=1, device_id=device, device_id_type=MESH)


def front_kernel(
    n_t, n_m, reach, absolute, audio_ref, table_ref, bank_ref, out_ref,
    rows, edge_sem, tm_send, mp_send, recv,
):
    t = lax.axis_index("tm")
    m = lax.axis_index("mp")
    own = out_ref.shape[2]
    stride = SUB * HOP // LANES
    flat = t * n_m + m
    has_prev = flat > 0
    has_next = flat < n_t * n_m - 1
    bits = bits_of(n_m)
    distances = []
    for d in range(1, reach + 1):
        distances += [d, -d]
    rows[pl.ds(0, own * stride), :] = audio_ref[...]
    rows[pl.ds(own * stride, 8), :] = jnp.zeros((8, LANES), F32)
    if not absolute:
        out_ref[...] = jnp.zeros_like(out_ref)

    barrier = pltpu.get_barrier_semaphore()

    def slot_of(distance):
        return t - distance if absolute else reach - distance

    for d in distances:
        inside = jnp.logical_and(t + d >= 0, t + d < n_t)

        @pl.when(inside)
        def _(d=d):
            signal(barrier, {"tm": t + d, "mp": m})

    for bit in bits:
        signal(barrier, {"tm": t, "mp": flipped(m, bit)})

    @pl.when(has_prev)
    def _():
        signal(barrier, beside(t, m, n_t, n_m, -1))

    @pl.when(has_next)
    def _():
        signal(barrier, beside(t, m, n_t, n_m, 1))

    peers = len(bits) + has_prev.astype(jnp.int32) + has_next.astype(jnp.int32)
    for d in distances:
        peers = peers + jnp.logical_and(t + d >= 0, t + d < n_t).astype(jnp.int32)
    pl.semaphore_wait(barrier, peers)

    def head_copy(device):
        return pltpu.make_async_remote_copy(
            src_ref=audio_ref.at[pl.ds(0, 8)],
            dst_ref=rows.at[pl.ds(own * stride, 8)],
            send_sem=edge_sem.at[0],
            recv_sem=edge_sem.at[1],
            device_id=device,
            device_id_type=MESH,
        )

    @pl.when(has_prev)
    def _():
        head_copy(beside(t, m, n_t, n_m, -1)).start()

    @pl.when(has_next)
    def _():
        head_copy(beside(t, m, n_t, n_m, 1)).wait_recv()

    pieces = [rows[pl.ds(j, own, stride=stride), :] for j in range(stride + 2)]
    frames = []
    for j in range(SUB):
        window = jnp.concatenate(pieces[j : j + WIN // LANES], axis=1)
        shift = (HOP - LANES) * j
        frames.append(pltpu.roll(window, WIN - shift, 1) if shift else window)
    spectrum = wide_dot(jnp.concatenate(frames, axis=0), table_ref)
    power = jnp.square(spectrum[:, :BINS]) + jnp.square(spectrum[:, BINS:])
    mel = jnp.log(wide_dot(power, bank_ref) + 1e-06).astype(BF16)
    here = slot_of(0)
    for j in range(SUB):
        out_ref[here, m, :, pl.ds(NMEL * j, NMEL)] = mel[j * own : (j + 1) * own]

    def tm_copy(d, slot, device):
        return pltpu.make_async_remote_copy(
            src_ref=out_ref.at[here, m],
            dst_ref=out_ref.at[slot, m],
            send_sem=tm_send.at[d + reach],
            recv_sem=recv.at[d + reach, 0],
            device_id=device,
            device_id_type=MESH,
        )

    def mp_copy(d, mask, bit):
        block = out_ref.at[slot_of(d), masked_index(m, mask)]
        return pltpu.make_async_remote_copy(
            src_ref=block,
            dst_ref=block,
            send_sem=mp_send.at[d + reach, mask + bit],
            recv_sem=recv.at[d + reach, mask + bit],
            device_id={"tm": t, "mp": flipped(m, bit)},
            device_id_type=MESH,
        )

    def forward(d, mask):
        for bit in reversed(bits):
            if bit < low_bit(mask, n_m):
                mp_copy(d, mask, bit).start()

    for d in distances:

        @pl.when(jnp.logical_and(t + d >= 0, t + d < n_t))
        def _(d=d):
            landing = t if absolute else reach - d
            tm_copy(d, landing, {"tm": t + d, "mp": m}).start()

    forward(0, 0)
    order = [0] + distances

    def when_held(d, body):
        if d == 0:
            body()
        else:
            pl.when(jnp.logical_and(t - d >= 0, t - d < n_t))(body)

    masks = sorted(range(1, n_m), key=lambda v: -low_bit(v, n_m))
    for d in distances:

        def arrive(d=d):
            landing = t if absolute else reach - d
            tm_copy(d, landing, {"tm": t, "mp": m}).wait_recv()
            forward(d, 0)

        when_held(d, arrive)
    for mask in masks:
        bit = low_bit(mask, n_m)
        for d in order:

            def relay(d=d, mask=mask, bit=bit):
                mp_copy(d, mask - bit, bit).wait_recv()
                forward(d, mask)

            when_held(d, relay)
    for d in distances:

        @pl.when(jnp.logical_and(t + d >= 0, t + d < n_t))
        def _(d=d):
            landing = t if absolute else reach - d
            tm_copy(d, landing, {"tm": t + d, "mp": m}).wait_send()

    for mask in range(1, n_m):
        bit = low_bit(mask, n_m)
        for d in order:

            def drain(d=d, mask=mask, bit=bit):
                mp_copy(d, mask - bit, bit).wait_send()

            when_held(d, drain)

    @pl.when(has_prev)
    def _():
        head_copy(beside(t, m, n_t, n_m, -1)).wait_send()


def heads_kernel(
    n_t, n_m, reach, absolute, place_ref, stacked_ref, start_ref, finish_ref, wsub_ref, watt_ref,
    wout_ref, part_ref, own_ref, feats, query, keys, values, attended,
):
    t = place_ref[0]
    m = place_ref[1]
    slots = stacked_ref.shape[0]
    own = stacked_ref.shape[2]
    shard = n_m * own
    width = watt_ref.shape[2]
    heads = width // HD
    mine = t if absolute else reach
    dot = functools.partial(jnp.dot, preferred_element_type=F32)
    for slot in range(slots):
        block = stacked_ref[slot].reshape(shard, SUB * NMEL)
        features = dot(block, wsub_ref[...]).astype(BF16)
        feats[pl.ds(slot * shard, shard), :] = features
        normed = normalize(features.astype(F32)).astype(BF16)
        keys[pl.ds(slot * shard, shard), :] = dot(normed, watt_ref[1]).astype(BF16)
        values[pl.ds(slot * shard, shard), :] = dot(normed, watt_ref[2]).astype(BF16)

        @pl.when(mine == slot)
        def _(normed=normed):
            asked = dot(normed, watt_ref[0]).astype(BF16)
            query[...] = (asked.astype(F32) * (1.0 / math.sqrt(HD))).astype(BF16)

    own_row = pl.multiple_of(mine * shard + m * own, own)
    own_ref[...] = feats[pl.ds(own_row, own), :]
    count = slots * shard
    begin = 0 if absolute else (t - reach) * shard
    position = lax.broadcasted_iota(jnp.int32, (shard, count), 1) + begin

    def column(ref):
        wide = jnp.broadcast_to(ref[...].astype(F32), (LANES, shard))
        return jnp.transpose(wide)[:, :1].astype(jnp.int32)

    allowed = jnp.logical_and(position >= column(start_ref), position < column(finish_ref))
    for head in range(heads):
        cut = slice(head * HD, (head + 1) * HD)
        scores = lax.dot_general(
            query[:, cut], keys[:, cut], (((1,), (1,)), ((), ())), preferred_element_type=F32
        )
        scores = jnp.where(allowed, scores, -1e30)
        weights = jnp.exp(scores - jnp.max(scores, axis=-1, keepdims=True))
        total = jnp.sum(weights, axis=-1, keepdims=True)
        attended[:, cut] = (dot(weights.astype(BF16), values[:, cut]) / total).astype(BF16)
    part_ref[...] = dot(attended[...], wout_ref[...]).astype(BF16)


def tail_kernel(
    n_t, n_m, part_ref, feature_ref, gain_ref, taps_ref, out_ref,
    landed, outgoing, mixed, edges, padded, part_send, part_recv, edge_send, edge_recv,
):
    t = lax.axis_index("tm")
    m = lax.axis_index("mp")
    own, width = feature_ref.shape
    flat = t * n_m + m
    has_prev = flat > 0
    has_next = flat < n_t * n_m - 1
    bits = bits_of(n_m)
    barrier = pltpu.get_barrier_semaphore()
    for bit in bits:
        signal(barrier, {"tm": t, "mp": flipped(m, bit)})

    @pl.when(has_prev)
    def _():
        signal(barrier, beside(t, m, n_t, n_m, -1))

    @pl.when(has_next)
    def _():
        signal(barrier, beside(t, m, n_t, n_m, 1))

    peers = len(bits) + has_prev.astype(jnp.int32) + has_next.astype(jnp.int32)
    pl.semaphore_wait(barrier, peers)

    def part_rows(mask):
        return pl.ds(pl.multiple_of(masked_index(m, mask) * own, own), own)

    slot_index = {}
    for bit in bits:
        for mask in range(n_m):
            if mask % (2 * bit) == 0:
                slot_index[bit, mask] = len(slot_index)

    def part_copy(bit, mask):
        index = slot_index[bit, mask]
        source = part_ref.at[part_rows(mask + bit)] if bit == 1 else outgoing.at[mask + bit]
        return pltpu.make_async_remote_copy(
            src_ref=source,
            dst_ref=landed.at[index],
            send_sem=part_send.at[index],
            recv_sem=part_recv.at[index],
            device_id={"tm": t, "mp": flipped(m, bit)},
            device_id_type=MESH,
        )

    total = {}
    for bit in bits:
        kept = [mask for mask in range(n_m) if mask % (2 * bit) == 0]
        kept = kept[::-1]
        if bit == 1:
            for mask in kept:
                part_copy(bit, mask).start()
        for mask in kept:
            part_copy(bit, mask).wait_recv()
            if bit == 1:
                base = part_ref[part_rows(mask), :].astype(F32)
            else:
                base = total[mask]
            total[mask] = base + landed[slot_index[bit, mask]].astype(F32)
            after = 2 * bit
            if mask % (2 * after) == after and after < n_m:
                outgoing[mask] = total[mask].astype(BF16)
                part_copy(after, mask - after).start()
    branch = total[0] if total else part_ref[...].astype(F32)
    blended = (feature_ref[...].astype(F32) + branch).astype(BF16)
    mixed[...] = blended
    normed = (normalize(blended.astype(F32)) * gain_ref[...]).astype(BF16)
    edges[0] = normed[:EDGE]
    edges[1] = normed[own - EDGE :]

    def edge_copy(side):
        return pltpu.make_async_remote_copy(
            src_ref=edges.at[side],
            dst_ref=edges.at[2 + side],
            send_sem=edge_send.at[side],
            recv_sem=edge_recv.at[side],
            device_id=beside(t, m, n_t, n_m, 2 * side - 1),
            device_id_type=MESH,
        )

    @pl.when(has_prev)
    def _():
        edge_copy(0).start()

    @pl.when(has_next)
    def _():
        edge_copy(1).start()

    padded[pl.ds(EDGE, own), :] = normed.astype(F32)
    padded[pl.ds(0, EDGE), :] = jnp.zeros((EDGE, width), F32)
    padded[pl.ds(EDGE + own, EDGE), :] = jnp.zeros((EDGE, width), F32)

    @pl.when(has_next)
    def _():
        edge_copy(0).wait_recv()
        padded[pl.ds(EDGE + own, EDGE), :] = edges[2].astype(F32)

    @pl.when(has_prev)
    def _():
        edge_copy(1).wait_recv()
        padded[pl.ds(0, EDGE), :] = edges[3].astype(F32)

    offset = EDGE - KERNEL // 2

    @pl.loop(0, width // LANES)
    def _(chunk):
        cols = pl.ds(pl.multiple_of(chunk * LANES, LANES), LANES)
        taps = taps_ref[:, cols].astype(F32)
        convolved = jnp.zeros((own, LANES), F32)
        for tap in range(KERNEL):
            convolved = convolved + padded[pl.ds(offset + tap, own), cols] * taps[tap : tap + 1]
        gated = convolved / (1.0 + jnp.exp(-convolved))
        out_ref[:, cols] = (mixed[:, cols].astype(F32) + gated).astype(BF16)

    for bit in bits:
        for mask in range(n_m):
            if mask % (2 * bit) == 0:
                part_copy(bit, mask).wait_send()

    @pl.when(has_prev)
    def _():
        edge_copy(0).wait_send()

    @pl.when(has_next)
    def _():
        edge_copy(1).wait_send()


VMEM = pl.BlockSpec(memory_space=pltpu.VMEM)
SMEM = pl.BlockSpec(memory_space=pltpu.SMEM)


def shards(
    n_t, n_m, waveform, segment_start, segment_end, w_subsample, w_attention, w_output,
    gain_convolution, w_depthwise,
):
    own = waveform.shape[0] // (SUB * HOP)
    shard = segment_start.shape[0]
    stacked_width, width = w_subsample.shape
    local = w_attention.shape[2]
    reach = min((SEG_MAX - 2) // shard + 1, n_t - 1)
    absolute = 2 * reach + 1 >= n_t
    slots = n_t if absolute else 2 * reach + 1
    lines = own * SUB * HOP // LANES
    audio = waveform.reshape(lines, LANES)
    dma = pltpu.SemaphoreType.DMA
    stacked = pl.pallas_call(
        functools.partial(front_kernel, n_t, n_m, reach, absolute),
        out_shape=jax.ShapeDtypeStruct((slots, n_m, own, stacked_width), BF16),
        in_specs=[VMEM] * 3,
        out_specs=VMEM,
        scratch_shapes=[
            pltpu.VMEM((lines + 8, LANES), F32),
            dma((2,)),
            dma((2 * reach + 1,)),
            dma((2 * reach + 1, n_m)),
            dma((2 * reach + 1, n_m)),
        ],
        compiler_params=pltpu.CompilerParams(collective_id=0, has_side_effects=True),
        name="front",
    )(audio, jnp.asarray(halves(fourier_table())), jnp.asarray(halves(mel_bank())))
    place = jnp.stack([lax.axis_index("tm"), lax.axis_index("mp")]).astype(jnp.int32)
    part, features = pl.pallas_call(
        functools.partial(heads_kernel, n_t, n_m, reach, absolute),
        out_shape=(
            jax.ShapeDtypeStruct((shard, width), BF16),
            jax.ShapeDtypeStruct((own, width), BF16),
        ),
        in_specs=[SMEM] + [VMEM] * 6,
        out_specs=(VMEM, VMEM),
        scratch_shapes=[
            pltpu.VMEM((slots * shard, width), BF16),
            pltpu.VMEM((shard, local), BF16),
            pltpu.VMEM((slots * shard, local), BF16),
            pltpu.VMEM((slots * shard, local), BF16),
            pltpu.VMEM((shard, local), BF16),
        ],
        name="heads",
    )(
        place, stacked, segment_start.reshape(1, shard), segment_end.reshape(1, shard),
        w_subsample, w_attention, w_output,
    )
    landings = max(n_m - 1, 1)
    return pl.pallas_call(
        functools.partial(tail_kernel, n_t, n_m),
        out_shape=jax.ShapeDtypeStruct((own, width), BF16),
        in_specs=[VMEM] * 4,
        out_specs=VMEM,
        scratch_shapes=[
            pltpu.VMEM((landings, own, width), BF16),
            pltpu.VMEM((n_m, own, width), BF16),
            pltpu.VMEM((own, width), BF16),
            pltpu.VMEM((4, EDGE, width), BF16),
            pltpu.VMEM((own + 2 * EDGE, width), F32),
            dma((landings,)),
            dma((landings,)),
            dma((2,)),
            dma((2,)),
        ],
        compiler_params=pltpu.CompilerParams(collective_id=1, has_side_effects=True),
        name="tail",
    )(part, features, gain_convolution.reshape(1, width), w_depthwise)


def solution(mesh):
    placed = (
        P(("groups", "tm", "mp")),
        P(("groups", "tm")),
        P(("groups", "tm")),
        P(),
        P(None, None, "mp"),
        P("mp", None),
        P(),
        P(),
    )
    return jax.shard_map(
        functools.partial(shards, mesh.shape["tm"], mesh.shape["mp"]),
        mesh=mesh,
        in_specs=placed,
        out_specs=P(("groups", "tm", "mp"), None),
        check_vma=False,
    )
```

time: 144 us -> 57.4 us (0.40); the launches traced: 142 us -> 57.2 us
  Pallas kernels: 0 us -> 54.3 us
  waiting for transfers between devices: 43.4 us -> 0 us
  starting transfers between devices: 25.8 us -> 0 us
  other arithmetic: 18.7 us -> 0.66 us
  local copies, waits for them, and re-layouts: 17.6 us -> 2.22 us
  matrix products: 15 us -> 0 us
  between operations: 14.1 us -> 0.03 us
  blocking collectives: 7.34 us -> 0 us
    pallas_call x0 -> x3, Pallas kernels: none -> 54.3 us  [the longest x1 22.4 us: shards(): pl.pallas_call(functools.partial(front_kernel, n_t, n_m, reach, absolute)...]
    ppermute x9 -> x0, starting transfers between devices: 25.8 us -> none  [the longest x7 21.2 us: shifted(): return lax.ppermute(block, axis, route)]
    ppermute x9 -> x0, waiting for transfers between devices: 24.2 us -> none  [the longest x7 22.1 us: shifted(): return lax.ppermute(block, axis, route)]
    reduce_scatter x1 -> x0, waiting for transfers between devices: 19.2 us -> none  [shards(): lax.psum_scatter(jnp.dot(attended, w_output, preferred_element_type=jnp.f...]
    dot_general x19 -> x0, matrix products: 15 us -> none  [the longest x7 3.13 us: fold_keys(): jnp.einsum('qhd,khd->qhk', queries, key_block, preferred_element_type=jnp...]
    slice x14 -> x0, local copies, waits for them, and re-layouts: 10.2 us -> none  [the longest x4 6.98 us: frame_rows(): blocks[offset:offset + frame_count]]
    all_gather x1 -> x0, blocking collectives: 7.34 us -> none  [shards(): all_stacked = lax.all_gather(stacked, 'mp', axis=0, tiled=True)]
    mul x4 -> x0, other arithmetic: 6.79 us -> none  [the longest x2 3.57 us: shards(): haloed[tap_index:tap_index + frames_local].astype(jnp.float32)]
  transfers between devices with their start and end apart: 10 -> 0, of which waited for: 3 -> 0; matrix products, arithmetic and copies ran while one was open for 11% -> 0% of each run, Pallas kernels for 0% -> 0%
where the time goes in v1:
time: 57.4 us; the launch traced here: 57.2 us
  Pallas kernels  54.3 us (95%)
  local copies, waits for them, and re-layouts  2.22 us (4%)
  other arithmetic  0.66 us (1%)
    pallas_call x1, Pallas kernels, shards(): pl.pallas_call(functools.partial(front_kernel, n_t, n_m, reach, absolute)...  22.4 us
    pallas_call x1, Pallas kernels, shards(): pl.pallas_call(functools.partial(heads_kernel, n_t, n_m, reach, absolute)...  16.6 us
    pallas_call x1, Pallas kernels, shards(): pl.pallas_call(functools.partial(tail_kernel, n_t, n_m), out_shape=jax.Sh...  15.3 us
    unnamed x3, local copies, waits for them, and re-layouts  1.62 us

profile of v1, /device:TPU:1, one launch (start us, length us, event | category | flops | bytes accessed | tf_op | source)
XLA Modules:
  0.0 57.2 jit_solution(11808384429898972550)
XLA Ops:
  0.0 0.7 %pad_add_fusion.place_ref = s32[2]{0:T(128)} fusion(s32[1]{0:T(128)} %bitcast.1, s32[1]{0:T(128)} %bitcast), kind=kLoop, calls=%fused_computation | loop fusion | flops 2 | bytes 16 | tf_op jit(solution)/shard_map/stack | solution.py:483
  0.7 22.4 %front.1.stacked_ref = bf16[4,4,64,512]{3,2,1,0:T(8,128)(2,1)} custom-call(f32[320,128]{1,0:T(8,128)} %bitcast.5, bf16[2,512,512]{2,1,0:T(8,128)(2,1)} %constant.11.clone.table_ref, bf16[2,256,128]{2,1,0:T(8,128)(2,1)} %constant.12.clone.bank_ref), custom_call_target="tpu_custom_call" | custom-call | tf_op jit(solution)/shard_map/front/pallas_call | solution.py:468
  23.1 0.0 copy-start
  23.1 16.6 %heads.1 = (bf16[256,1536]{1,0:T(8,128)(2,1)}, bf16[64,1536]{1,0:T(8,128)(2,1)}) custom-call(s32[2]{0:T(128)} %pad_add_fusion.place_ref, bf16[4,4,64,512]{3,2,1,0:T(8,128)(2,1)} %front.1.stacked_ref, s32[1,256]{1,0:T(1,128)} %bitcast.6, s32[1,256]{1,0:T(1,128)} %bitcast.7, bf16[512,1536]{1,0:T(8,128)(2,1)} %wsub_ref.1, bf16[3,1536,384]{2,1,0:T(8,128)(2,1)} %watt_ref.1, ...), custom_call_target="tpu_custom_call" | custom-call | tf_op jit(solution)/shard_map/heads/pallas_call | solution.py:484
  39.7 0.0 copy-done
  39.7 0.6 %reshape.15.gain_ref = f32[1,1536]{1,0:T(1,128)} reshape(f32[1536]{0:T(1024)S(1)} %copy-done) | data formatting | bytes 12288 | tf_op jit(solution)/shard_map/reshape | solution.py:523
  40.3 15.3 %tail.1 = bf16[64,1536]{1,0:T(8,128)(2,1)} custom-call(bf16[256,1536]{1,0:T(8,128)(2,1)} %get-tuple-element.7.part_ref, bf16[64,1536]{1,0:T(8,128)(2,1)} %get-tuple-element.8.feature_ref, f32[1,1536]{1,0:T(1,128)} %reshape.15.gain_ref, bf16[31,1536]{1,0:T(8,128)(2,1)} %taps_ref.1), custom_call_target="tpu_custom_call" | custom-call | tf_op jit(solution)/shard_map/tail/pallas_call | solution.py:505
  55.6 1.6 %copy.12 = bf16[64,1536]{1,0:T(8,128)(2,1)} copy(bf16[64,1536]{1,0:T(8,128)(2,1)} %tail.1) | data formatting | bytes 393216
Async XLA Ops:
  23.1 16.6 %copy-start = (f32[1536]{0:T(1024)S(1)}, f32[1536]{0:T(1024)}, u32[]{:S(2)}) copy-start(f32[1536]{0:T(1024)} %param.16) | copy-start | bytes 18436

commit v2 on v1

v2 whole, which is shorter than its diff:
```python
import functools
import math

import jax
import jax.numpy as jnp
import numpy as np
from jax import lax
from jax.experimental import pallas as pl
from jax.experimental.pallas import tpu as pltpu
from jax.sharding import PartitionSpec as P

HD = 64
NMEL = 128
NFFT = 400
HOP = 160
BINS = 256
SUB = 4
KERNEL = 31
SEG_MAX = 750
LANES = 128
WIN = 512
EDGE = 16
MESH = pl.DeviceIdType.MESH
F32 = jnp.float32
BF16 = jnp.bfloat16


def fourier_table():
    sample_index = np.arange(NFFT)[:, None]
    bin_index = np.arange(BINS)[None, :]
    angle = (sample_index * bin_index % NFFT) * (2.0 * math.pi / NFFT)
    window = 0.5 - 0.5 * np.cos(np.arange(NFFT) * (2.0 * math.pi / NFFT))
    kept = bin_index <= NFFT // 2
    cosine = np.where(kept, np.cos(angle), 0.0) * window[:, None]
    sine = np.where(kept, -np.sin(angle), 0.0) * window[:, None]
    table = np.concatenate([cosine, sine], axis=1)
    return np.concatenate([table, np.zeros((WIN - NFFT, 2 * BINS))], axis=0)


def mel_bank():
    mel_top = 2595.0 * math.log10(1.0 + 8000.0 / 700.0)
    points = np.arange(NMEL + 2) * (mel_top / (NMEL + 1))
    edges = 700.0 * (np.power(10.0, points / 2595.0) - 1.0) * (NFFT / 16000.0)
    centers = edges[1:-1]
    widths = np.maximum(edges[2:] - edges[1:-1], 1.0)
    bins = np.arange(BINS)[:, None]
    triangle = np.maximum(0.0, 1.0 - np.abs(bins - centers[None, :]) / widths[None, :])
    return np.where(bins <= NFFT // 2, triangle, 0.0)


def halves(values):
    values = values.astype(np.float32)
    high = values.astype(BF16)
    low = (values - high.astype(np.float32)).astype(BF16)
    return np.stack([high, low])


def split(values):
    high = values.astype(BF16)
    return high, (values - high.astype(F32)).astype(BF16)


def wide_dot(values, table):
    high, low = split(values)
    dot = functools.partial(jnp.dot, preferred_element_type=F32)
    return dot(high, table[0]) + (dot(high, table[1]) + dot(low, table[0]))


def flipped(index, bit):
    return index + bit - 2 * bit * ((index // bit) % 2)


def masked_index(index, mask):
    bit = 1
    while bit <= mask:
        if mask & bit:
            index = flipped(index, bit)
        bit *= 2
    return index


def bits_of(count):
    bits = []
    bit = 1
    while bit < count:
        bits.append(bit)
        bit *= 2
    return bits


def low_bit(mask, count):
    return mask & -mask if mask else count


def normalize(values):
    center = jnp.mean(values, axis=-1, keepdims=True)
    shifted = values - center
    spread = jnp.mean(jnp.square(shifted), axis=-1, keepdims=True)
    return shifted * lax.rsqrt(spread + 1e-05)


def beside(t, m, n_t, n_m, step):
    flat = t * n_m + m + step
    return {"tm": flat // n_m, "mp": flat % n_m}


def signal(sem, device):
    pl.semaphore_signal(sem, inc=1, device_id=device, device_id_type=MESH)


def block_kernel(
    n_t, n_m, reach, absolute, audio_ref, table_ref, bank_ref, start_ref, finish_ref, gain_ref, taps_ref,
    wsub_hbm, watt_hbm, wout_hbm, out_ref,
    rows, gathered, wsub, watt, wout, folded, query, keys, values, bounds, features, parts, landed, outgoing,
    edges, padded, load_sem, head_sem, tm_send, mp_send, recv, part_send, part_recv, edge_send, edge_recv,
):
    t = lax.axis_index("tm")
    m = lax.axis_index("mp")
    slots, _, own, stacked_width = gathered.shape
    shard = n_m * own
    width = out_ref.shape[1]
    local = watt.shape[2]
    count = slots * shard
    stride = SUB * HOP // LANES
    flat = t * n_m + m
    has_prev = flat > 0
    has_next = flat < n_t * n_m - 1
    bits = bits_of(n_m)
    distances = []
    for d in range(1, reach + 1):
        distances += [d, -d]
    dot = functools.partial(jnp.dot, preferred_element_type=F32)
    here = t if absolute else reach
    prev_device = beside(t, m, n_t, n_m, -1)
    next_device = beside(t, m, n_t, n_m, 1)

    loads = [pltpu.make_async_copy(wsub_hbm, wsub.at[pl.ds(0, stacked_width)], load_sem.at[0])]
    for k in range(3):
        loads.append(pltpu.make_async_copy(watt_hbm.at[k], watt.at[k], load_sem.at[1 + k]))
    loads.append(pltpu.make_async_copy(wout_hbm, wout, load_sem.at[4]))
    for load in loads:
        load.start()

    rows[pl.ds(0, own * stride), :] = audio_ref[...]
    rows[pl.ds(own * stride, 8), :] = jnp.zeros((8, LANES), F32)
    if not absolute:
        gathered[...] = jnp.zeros_like(gathered)
    barrier = pltpu.get_barrier_semaphore()
    peers = len(bits) + has_prev.astype(jnp.int32) + has_next.astype(jnp.int32)
    for d in distances:
        inside = jnp.logical_and(t + d >= 0, t + d < n_t)
        peers = peers + inside.astype(jnp.int32)

        @pl.when(inside)
        def _(d=d):
            signal(barrier, {"tm": t + d, "mp": m})

    for bit in bits:
        signal(barrier, {"tm": t, "mp": flipped(m, bit)})

    @pl.when(has_prev)
    def _():
        signal(barrier, prev_device)

    @pl.when(has_next)
    def _():
        signal(barrier, next_device)

    for index, ref in enumerate((start_ref, finish_ref)):
        wide = jnp.broadcast_to(ref[...].astype(F32), (LANES, shard))
        bounds[index] = jnp.transpose(wide).astype(jnp.int32)
    wsub[pl.ds(stacked_width, EDGE), :] = jnp.ones((EDGE, width), BF16)
    pl.semaphore_wait(barrier, peers)

    def head_copy(device):
        return pltpu.make_async_remote_copy(
            src_ref=audio_ref.at[pl.ds(0, 8)],
            dst_ref=rows.at[pl.ds(own * stride, 8)],
            send_sem=head_sem.at[0],
            recv_sem=head_sem.at[1],
            device_id=device,
            device_id_type=MESH,
        )

    @pl.when(has_prev)
    def _():
        head_copy(prev_device).start()

    def fold(k, scale):
        loads[1 + k].wait()
        product = dot(wsub[...], watt[k])
        center = jnp.mean(wsub[pl.ds(0, stacked_width), :].astype(F32), axis=-1, keepdims=True)
        centered = product[:stacked_width] - center * product[stacked_width : stacked_width + 1]
        folded[k] = (centered * scale).astype(BF16)

    loads[0].wait()
    fold(0, 1.0 / math.sqrt(HD))

    @pl.when(has_next)
    def _():
        head_copy(next_device).wait_recv()

    pieces = [rows[pl.ds(j, own, stride=stride), :] for j in range(stride + 2)]
    frames = []
    for j in range(SUB):
        window = jnp.concatenate(pieces[j : j + WIN // LANES], axis=1)
        shift = (HOP - LANES) * j
        frames.append(pltpu.roll(window, WIN - shift, 1) if shift else window)
    spectrum = wide_dot(jnp.concatenate(frames, axis=0), table_ref)
    power = jnp.square(spectrum[:, :BINS]) + jnp.square(spectrum[:, BINS:])
    mel = jnp.log(wide_dot(power, bank_ref) + 1e-06).astype(BF16)
    stacked = jnp.concatenate([mel[j * own : (j + 1) * own] for j in range(SUB)], axis=1)
    mapped = dot(stacked, wsub[pl.ds(0, stacked_width), :]).astype(BF16)
    features[...] = mapped
    shifted = mapped.astype(F32)
    shifted = shifted - jnp.mean(shifted, axis=-1, keepdims=True)
    spread = jnp.mean(jnp.square(shifted), axis=-1, keepdims=True)
    gathered[here, m] = (stacked.astype(F32) * lax.rsqrt(spread + 1e-05)).astype(BF16)

    def tm_copy(d):
        return pltpu.make_async_remote_copy(
            src_ref=gathered.at[here, m],
            dst_ref=gathered.at[t if absolute else reach - d, m],
            send_sem=tm_send.at[d + reach],
            recv_sem=recv.at[d + reach, 0],
            device_id={"tm": t + d, "mp": m},
            device_id_type=MESH,
        )

    def slot_of(d):
        return t - d if absolute else reach - d

    def mp_copy(d, mask, bit):
        block = gathered.at[slot_of(d), masked_index(m, mask)]
        return pltpu.make_async_remote_copy(
            src_ref=block,
            dst_ref=block,
            send_sem=mp_send.at[d + reach, mask + bit],
            recv_sem=recv.at[d + reach, mask + bit],
            device_id={"tm": t, "mp": flipped(m, bit)},
            device_id_type=MESH,
        )

    def forward(d, mask):
        for bit in reversed(bits):
            if bit < low_bit(mask, n_m):
                mp_copy(d, mask, bit).start()

    def when_sent(d, body):
        pl.when(jnp.logical_and(t + d >= 0, t + d < n_t))(body)

    def when_held(d, body):
        if d == 0:
            body()
        else:
            pl.when(jnp.logical_and(t - d >= 0, t - d < n_t))(body)

    def arrive(d):
        def body():
            tm_copy(d).wait_recv()
            forward(d, 0)

        when_held(d, body)

    def relay(d, mask):
        def body():
            bit = low_bit(mask, n_m)
            mp_copy(d, mask - bit, bit).wait_recv()
            forward(d, mask)

        when_held(d, body)

    def project(slot, asking):
        block = gathered[slot].reshape(shard, stacked_width)
        place = pl.ds(pl.multiple_of(slot * shard, shard), shard)
        if asking:
            query[...] = dot(block, folded[0]).astype(BF16)
        keys[place, :] = dot(block, folded[1]).astype(BF16)
        values[place, :] = dot(block, folded[2]).astype(BF16)

    for d in distances:
        when_sent(d, lambda d=d: tm_copy(d).start())
    forward(0, 0)
    fold(1, 1.0)
    for d in distances[:2]:
        arrive(d)
    fold(2, 1.0)
    for d in distances[2:]:
        arrive(d)
    masks = sorted(range(1, n_m), key=lambda v: -low_bit(v, n_m))
    passing = [mask for mask in masks if mask % 2 == 0]
    ending = [mask for mask in masks if mask % 2]
    for mask in passing:
        relay(0, mask)
    for d in distances[:2]:
        for mask in passing:
            relay(d, mask)
    for mask in ending:
        relay(0, mask)
    project(here, True)
    for d in distances[2:]:
        for mask in passing:
            relay(d, mask)
    for d in distances:
        for mask in ending:
            relay(d, mask)
    for step in range(1, slots):
        project((here + step) % slots, False)

    begin = 0 if absolute else (t - reach) * shard
    loads[4].wait()

    def chunk_rows(mask):
        return pl.ds(pl.multiple_of(masked_index(m, mask) * own, own), own)

    def branch_of(group):
        tall = own * len(group)
        asked = jnp.concatenate([query[chunk_rows(mask), :] for mask in group], axis=0)
        first = jnp.concatenate([bounds[0, chunk_rows(mask), :] for mask in group], axis=0)[:, :1]
        last = jnp.concatenate([bounds[1, chunk_rows(mask), :] for mask in group], axis=0)[:, :1]
        position = lax.broadcasted_iota(jnp.int32, (tall, count), 1) + begin
        allowed = jnp.logical_and(position >= first, position < last)
        mixed_heads = []
        for head in range(local // HD):
            cut = slice(head * HD, (head + 1) * HD)
            scores = lax.dot_general(
                asked[:, cut], keys[:, cut], (((1,), (1,)), ((), ())), preferred_element_type=F32
            )
            scores = jnp.where(allowed, scores, -1e30)
            weights = jnp.exp(scores - jnp.max(scores, axis=-1, keepdims=True))
            total = jnp.sum(weights, axis=-1, keepdims=True)
            mixed_heads.append((dot(weights.astype(BF16), values[:, cut]) / total).astype(BF16))
        return dot(jnp.concatenate(mixed_heads, axis=1), wout[...]).astype(BF16)

    slot_index = {}
    for bit in bits:
        for mask in range(n_m):
            if mask % (2 * bit) == 0:
                slot_index[bit, mask] = len(slot_index)

    def part_copy(bit, mask):
        index = slot_index[bit, mask]
        return pltpu.make_async_remote_copy(
            src_ref=parts.at[mask + bit],
            dst_ref=landed.at[index],
            send_sem=part_send.at[index],
            recv_sem=part_recv.at[index],
            device_id={"tm": t, "mp": flipped(m, bit)},
            device_id_type=MESH,
        )

    odd = [mask for mask in range(n_m) if mask % 2][::-1]
    if odd:
        branches = branch_of(odd)
        for place, mask in enumerate(odd):
            parts[mask] = branches[place * own : (place + 1) * own]
            part_copy(1, mask - 1).start()
    total = None
    for mask in [v for v in range(n_m) if v % 2 == 0][::-1]:
        total = branch_of([mask]).astype(F32)
        for bit in bits:
            if mask % (2 * bit) == 0:
                part_copy(bit, mask).wait_recv()
                total = total + landed[slot_index[bit, mask]].astype(F32)
        if mask:
            parts[mask] = total.astype(BF16)
            low = low_bit(mask, n_m)
            part_copy(low, mask - low).start()
    blended = (features[...].astype(F32) + total).astype(BF16)
    outgoing[...] = blended
    normed = (normalize(blended.astype(F32)) * gain_ref[...]).astype(BF16)
    edges[0] = normed[:EDGE]
    edges[1] = normed[own - EDGE :]

    def edge_copy(side):
        return pltpu.make_async_remote_copy(
            src_ref=edges.at[side],
            dst_ref=edges.at[2 + side],
            send_sem=edge_send.at[side],
            recv_sem=edge_recv.at[side],
            device_id=next_device if side else prev_device,
            device_id_type=MESH,
        )

    @pl.when(has_prev)
    def _():
        edge_copy(0).start()

    @pl.when(has_next)
    def _():
        edge_copy(1).start()

    padded[pl.ds(EDGE, own), :] = normed.astype(F32)
    padded[pl.ds(0, EDGE), :] = jnp.zeros((EDGE, width), F32)
    padded[pl.ds(EDGE + own, EDGE), :] = jnp.zeros((EDGE, width), F32)

    @pl.when(has_next)
    def _():
        edge_copy(0).wait_recv()
        padded[pl.ds(EDGE + own, EDGE), :] = edges[2].astype(F32)

    @pl.when(has_prev)
    def _():
        edge_copy(1).wait_recv()
        padded[pl.ds(0, EDGE), :] = edges[3].astype(F32)

    offset = EDGE - KERNEL // 2

    @pl.loop(0, width // LANES)
    def _(chunk):
        cols = pl.ds(pl.multiple_of(chunk * LANES, LANES), LANES)
        taps = taps_ref[:, cols].astype(F32)
        convolved = jnp.zeros((own, LANES), F32)
        for tap in range(KERNEL):
            convolved = convolved + padded[pl.ds(offset + tap, own), cols] * taps[tap : tap + 1]
        gated = convolved / (1.0 + jnp.exp(-convolved))
        out_ref[:, cols] = (outgoing[:, cols].astype(F32) + gated).astype(BF16)

    for d in distances:
        when_sent(d, lambda d=d: tm_copy(d).wait_send())
    for mask in range(1, n_m):
        bit = low_bit(mask, n_m)
        for d in [0] + distances:
            when_held(d, lambda d=d, mask=mask, bit=bit: mp_copy(d, mask - bit, bit).wait_send())
    for bit, mask in slot_index:
        part_copy(bit, mask).wait_send()

    @pl.when(has_prev)
    def _():
        head_copy(prev_device).wait_send()
        edge_copy(0).wait_send()

    @pl.when(has_next)
    def _():
        edge_copy(1).wait_send()


VMEM = pl.BlockSpec(memory_space=pltpu.VMEM)
HBM = pl.BlockSpec(memory_space=pl.ANY)


def shards(
    n_t, n_m, waveform, segment_start, segment_end, w_subsample, w_attention, w_output,
    gain_convolution, w_depthwise,
):
    own = waveform.shape[0] // (SUB * HOP)
    shard = segment_start.shape[0]
    stacked_width, width = w_subsample.shape
    local = w_attention.shape[2]
    reach = min((SEG_MAX - 2) // shard + 1, n_t - 1)
    absolute = 2 * reach + 1 >= n_t
    slots = n_t if absolute else 2 * reach + 1
    lines = own * SUB * HOP // LANES
    audio = waveform.reshape(lines, LANES)
    dma = pltpu.SemaphoreType.DMA
    spans = 2 * reach + 1
    landings = max(n_m - 1, 1)
    return pl.pallas_call(
        functools.partial(block_kernel, n_t, n_m, reach, absolute),
        out_shape=jax.ShapeDtypeStruct((own, width), BF16),
        in_specs=[VMEM] * 7 + [HBM] * 3,
        out_specs=VMEM,
        scratch_shapes=[
            pltpu.VMEM((lines + 8, LANES), F32),
            pltpu.VMEM((slots, n_m, own, stacked_width), BF16),
            pltpu.VMEM((stacked_width + EDGE, width), BF16),
            pltpu.VMEM((3, width, local), BF16),
            pltpu.VMEM((local, width), BF16),
            pltpu.VMEM((3, stacked_width, local), BF16),
            pltpu.VMEM((shard, local), BF16),
            pltpu.VMEM((slots * shard, local), BF16),
            pltpu.VMEM((slots * shard, local), BF16),
            pltpu.VMEM((2, shard, LANES), jnp.int32),
            pltpu.VMEM((own, width), BF16),
            pltpu.VMEM((n_m, own, width), BF16),
            pltpu.VMEM((landings, own, width), BF16),
            pltpu.VMEM((own, width), BF16),
            pltpu.VMEM((4, EDGE, width), BF16),
            pltpu.VMEM((own + 2 * EDGE, width), F32),
            dma((5,)),
            dma((2,)),
            dma((spans,)),
            dma((spans, n_m)),
            dma((spans, n_m)),
            dma((landings,)),
            dma((landings,)),
            dma((2,)),
            dma((2,)),
        ],
        compiler_params=pltpu.CompilerParams(collective_id=0, has_side_effects=True),
        name="block",
    )(
        audio, jnp.asarray(halves(fourier_table())), jnp.asarray(halves(mel_bank())),
        segment_start.reshape(1, shard), segment_end.reshape(1, shard), gain_convolution.reshape(1, width),
        w_depthwise, w_subsample, w_attention, w_output,
    )


def solution(mesh):
    placed = (
        P(("groups", "tm", "mp")),
        P(("groups", "tm")),
        P(("groups", "tm")),
        P(),
        P(None, None, "mp"),
        P("mp", None),
        P(),
        P(),
    )
    return jax.shard_map(
        functools.partial(shards, mesh.shape["tm"], mesh.shape["mp"]),
        mesh=mesh,
        in_specs=placed,
        out_specs=P(("groups", "tm", "mp"), None),
        check_vma=False,
    )
```

time: 57.4 us -> 45.6 us (0.79)
  Pallas kernels: 54.3 us -> 42.5 us
  local copies, waits for them, and re-layouts: 2.22 us -> 2.91 us
  other arithmetic: 0.66 us -> 0 us
    pallas_call x3 -> x1, Pallas kernels: 54.3 us -> 42.5 us  [shards(): pl.pallas_call(functools.partial(block_kernel, n_t, n_m, reach, absolute)...]
    reshape x1, local copies, waits for them, and re-layouts: 0.6 us -> 1.29 us  [shards(): gain_convolution.reshape(1, width)]
    another operation x1 -> x0, other arithmetic: 0.66 us -> none  [shards(): jnp.stack([lax.axis_index('tm'), lax.axis_index('mp')]).astype(jnp.int32)]
    unnamed x3 -> x1, local copies, waits for them, and re-layouts: 1.62 us -> 1.62 us
where the time goes in v2:
time: 45.6 us; the launch traced here: 45.4 us
  Pallas kernels  42.5 us (93%)
  local copies, waits for them, and re-layouts  2.91 us (6%)
    pallas_call x1, Pallas kernels, shards(): pl.pallas_call(functools.partial(block_kernel, n_t, n_m, reach, absolute)...  42.5 us
    unnamed x1, local copies, waits for them, and re-layouts  1.62 us
    reshape x1, local copies, waits for them, and re-layouts, shards(): gain_convolution.reshape(1, width)  1.29 us

profile of v2, /device:TPU:1, one launch (start us, length us, event | category | flops | bytes accessed | tf_op | source)
XLA Modules:
  0.0 45.4 jit_solution(11774995166688049837)
XLA Ops:
  0.0 1.3 %reshape.15.gain_ref = f32[1,1536]{1,0:T(1,128)} reshape(f32[1536]{0:T(1024)} %param.16) | data formatting | bytes 12288 | tf_op jit(solution)/shard_map/reshape | solution.py:494
  1.3 42.5 %block.1 = bf16[64,1536]{1,0:T(8,128)(2,1)} custom-call(f32[320,128]{1,0:T(8,128)} %bitcast.3, bf16[2,512,512]{2,1,0:T(8,128)(2,1)} %constant.4.clone.table_ref, bf16[2,256,128]{2,1,0:T(8,128)(2,1)} %constant.5.clone.bank_ref, s32[1,256]{1,0:T(1,128)} %bitcast.4, s32[1,256]{1,0:T(1,128)} %bitcast.5, f32[1,1536]{1,0:T(1,128)} %reshape.15.gain_ref, ...), custom_call_target="tpu_custom_call" | custom-call | tf_op jit(solution)/shard_map/block/pallas_call | solution.py:458
  43.8 1.6 %copy.12 = bf16[64,1536]{1,0:T(8,128)(2,1)} copy(bf16[64,1536]{1,0:T(8,128)(2,1)} %block.1) | data formatting | bytes 393216

commit v3 on v2

--- a/solution.py
+++ b/solution.py
@@ -278,7 +278,7 @@
         keys[place, :] = dot(block, folded[1]).astype(BF16)
         values[place, :] = dot(block, folded[2]).astype(BF16)
 
-    for d in distances:
+    for d in distances[::-1]:
         when_sent(d, lambda d=d: tm_copy(d).start())
     forward(0, 0)
     fold(1, 1.0)
@@ -349,26 +349,28 @@
             device_id_type=MESH,
         )
 
-    odd = [mask for mask in range(n_m) if mask % 2][::-1]
-    if odd:
-        branches = branch_of(odd)
-        for place, mask in enumerate(odd):
-            parts[mask] = branches[place * own : (place + 1) * own]
-            part_copy(1, mask - 1).start()
+    groups = [[mask] for mask in range(n_m)][:1:-1] + [list(range(min(n_m, 2)))[::-1]]
     total = None
-    for mask in [v for v in range(n_m) if v % 2 == 0][::-1]:
-        total = branch_of([mask]).astype(F32)
-        for bit in bits:
-            if mask % (2 * bit) == 0:
-                part_copy(bit, mask).wait_recv()
-                total = total + landed[slot_index[bit, mask]].astype(F32)
-        if mask:
-            parts[mask] = total.astype(BF16)
-            low = low_bit(mask, n_m)
-            part_copy(low, mask - low).start()
+    for group in groups:
+        branches = branch_of(group)
+        for place, mask in enumerate(group):
+            part = branches[place * own : (place + 1) * own]
+            if mask % 2:
+                parts[mask] = part
+                part_copy(1, mask - 1).start()
+                continue
+            total = part.astype(F32)
+            for bit in bits:
+                if mask % (2 * bit) == 0:
+                    part_copy(bit, mask).wait_recv()
+                    total = total + landed[slot_index[bit, mask]].astype(F32)
+            if mask:
+                parts[mask] = total.astype(BF16)
+                low = low_bit(mask, n_m)
+                part_copy(low, mask - low).start()
     blended = (features[...].astype(F32) + total).astype(BF16)
     outgoing[...] = blended
-    normed = (normalize(blended.astype(F32)) * gain_ref[...]).astype(BF16)
+    normed = (normalize(blended.astype(F32)) * gain_ref[...][None, :]).astype(BF16)
     edges[0] = normed[:EDGE]
     edges[1] = normed[own - EDGE :]
 
@@ -491,7 +493,7 @@
         name="block",
     )(
         audio, jnp.asarray(halves(fourier_table())), jnp.asarray(halves(mel_bank())),
-        segment_start.reshape(1, shard), segment_end.reshape(1, shard), gain_convolution.reshape(1, width),
+        segment_start.reshape(1, shard), segment_end.reshape(1, shard), gain_convolution,
         w_depthwise, w_subsample, w_attention, w_output,
     )
 

time: 45.6 us -> 43.6 us (0.956)
  local copies, waits for them, and re-layouts: 2.91 us -> 1.62 us
  Pallas kernels: 42.5 us -> 41.8 us
    reshape x1 -> x0, local copies, waits for them, and re-layouts: 1.29 us -> none  [shards(): gain_convolution.reshape(1, width)]
    pallas_call x1, Pallas kernels: 42.5 us -> 41.8 us  [shards(): pl.pallas_call(functools.partial(block_kernel, n_t, n_m, reach, absolute)...]
where the time goes in v3:
time: 43.6 us; the launch traced here: 43.5 us
  Pallas kernels  41.8 us (96%)
  local copies, waits for them, and re-layouts  1.62 us (4%)
    pallas_call x1, Pallas kernels, shards(): pl.pallas_call(functools.partial(block_kernel, n_t, n_m, reach, absolute)...  41.8 us
    unnamed x1, local copies, waits for them, and re-layouts  1.62 us

profile of v3, /device:TPU:1, one launch (start us, length us, event | category | flops | bytes accessed | tf_op | source)
XLA Modules:
  0.0 43.5 jit_solution(3533352839788727096)
XLA Ops:
  0.0 41.8 %block.1 = bf16[64,1536]{1,0:T(8,128)(2,1)} custom-call(f32[320,128]{1,0:T(8,128)} %bitcast.3, bf16[2,512,512]{2,1,0:T(8,128)(2,1)} %constant.4.clone.table_ref, bf16[2,256,128]{2,1,0:T(8,128)(2,1)} %constant.5.clone.bank_ref, s32[1,256]{1,0:T(1,128)} %bitcast.4, s32[1,256]{1,0:T(1,128)} %bitcast.5, f32[1536]{0:T(1024)} %gain_ref.1, ...), custom_call_target="tpu_custom_call" | custom-call | tf_op jit(solution)/shard_map/block/pallas_call | solution.py:460
  41.8 1.6 %copy.12 = bf16[64,1536]{1,0:T(8,128)(2,1)} copy(bf16[64,1536]{1,0:T(8,128)(2,1)} %block.1) | data formatting | bytes 393216
